TPU v7x, 128 devices: a whole 4x4x4 slice. The times are simulated.
128 devices in a mesh: dom: 16 (over y_hi, x, core), feat: 8 (over z, y_lo).
Axes of the slice: x: 4, y: 4 (y_hi: 2, y_lo: 2; y = y_hi * 2 + y_lo), z: 4, core: 2. Of those that a mesh axis runs over, the one named last changes fastest.
Arguments:
- state: bfloat16 [512, 32768], P('feat', 'dom'), may hold values from -3 to 3
- inputs: bfloat16 [2, 32768], P(None, 'dom'), may hold values from -6 to 6
- adj_tiles: bfloat16 [256, 4, 128, 128], P('dom'), may hold values from -0.25 to 0.25
- adj_cols: int32 [256, 4], P('dom'), may hold values from 0 to 17, as said below
- valid_rows: int32 [16], P('dom'), may hold values from 1024 to 2048, as said below
- cluster_of: int32 [32768], P('dom'), may hold values from 0 to 4095
- w_gates: bfloat16 [3, 512, 4, 512], P(None, 'feat'), may hold values from -0.125 to 0.125
- w_input: bfloat16 [3, 512, 2], P(None, 'feat'), may hold values from -4 to 4
- bias: float32 [3, 512], P(None, 'feat'), may hold values from -4 to 4
- w_value: bfloat16 [8, 64, 64], P('feat'), may hold values from -0.75 to 0.75
- source_emb: float32 [8, 10, 4096], P('feat'), may hold values from -5 to 5
- target_emb: float32 [8, 10, 4096], P('feat'), may hold values from -5 to 5
- coarse_tiles: bfloat16 [32, 2, 128, 128], replicated, may hold values from -0.375 to 0.375
- coarse_cols: int32 [32, 2], replicated, may hold values from 0 to 31
Outputs:
- new_state: bfloat16 [512, 32768], P('feat', 'dom')
Inputs may be any that keep to these rules, and one draw needn't show every extreme that they name: `adj_cols`: for local row tile t of a partition (t counted from 0 in the partition), every entry lies in t to t + 2, the first is t and the last is t + 2. `valid_rows`: some partition has all 2048 rows valid and another exactly half of them.
All inputs are finite; a program needn't handle non-finite values.
Results may differ from a plain program's by a relative error of at most 0.003.
Values may be sent and summed in bfloat16 or wider, within the bound.
A program may use at most 64 MiB of HBM per device.

v0:
```python
import math
import jax
import jax.numpy as jnp
from jax import lax
from jax.sharding import PartitionSpec as P


def extended_2(array, sides, width):
    for axis, dim in sides:
        peers, length = (lax.axis_size(axis), array.shape[dim])
        up = [(i, (i + 1) % peers) for i in range(peers)]
        down = [(j, i) for i, j in up]
        last = lax.slice_in_dim(array, length - width, length, axis=dim)
        leading = lax.slice_in_dim(array, 0, width, axis=dim)
        before = lax.ppermute(last, axis, up)
        after = lax.ppermute(leading, axis, down)
        array = jnp.concatenate([before, array, after], axis=dim)
    return array


def diffuse(states, adj_tiles, adj_cols, row_mask):
    tile_size = adj_tiles.shape[2]
    channels, row_count = states.shape
    extended = extended_2(states, (("dom", 1),), tile_size)
    extended = extended.reshape(channels, row_count // tile_size + 2, tile_size)
    picked = extended[:, adj_cols]
    result = jnp.einsum("hnkj,nkji->hni", picked, adj_tiles, preferred_element_type=jnp.float32)
    return (result.reshape(channels, row_count) * row_mask).astype(jnp.bfloat16)


def project(pooled, w_value):
    heads_here, head_size = (w_value.shape[0], w_value.shape[1])
    grouped = pooled.reshape(heads_here, head_size, pooled.shape[1])
    return jnp.einsum(
        "hde,hec->hdc", w_value.astype(jnp.float32), grouped, precision=lax.Precision.HIGHEST
    ).astype(jnp.bfloat16)


def attend(source_cols, target_emb, values):
    heads_here, emb_dim, query_count = source_cols.shape
    block_rows = math.gcd(query_count, 512)
    blocks = source_cols.reshape(heads_here, emb_dim, query_count // block_rows, block_rows)
    blocks = jnp.moveaxis(blocks, 2, 0)

    def one_block(source_block):
        scores = jnp.einsum(
            "hei,hej->hij", source_block, target_emb, precision=lax.Precision.HIGHEST
        )
        scores = jnp.maximum(scores, 0.0)
        row_peak = jnp.max(scores, axis=2, keepdims=True)
        raised = jnp.exp(scores - row_peak)
        weights = (raised / jnp.sum(raised, axis=2, keepdims=True)).astype(jnp.bfloat16)
        return jnp.einsum("hdj,hij->hdi", values, weights, preferred_element_type=jnp.float32)

    outputs = lax.map(one_block, blocks)
    outputs = jnp.moveaxis(outputs, 0, 2)
    return outputs.reshape(heads_here, values.shape[1], query_count)


def body(
    state,
    inputs,
    adj_tiles,
    adj_cols,
    valid_rows,
    cluster_of,
    w_gates,
    w_input,
    bias,
    w_value,
    source_emb,
    target_emb,
    coarse_tiles,
    coarse_cols,
):
    channels, row_count = state.shape
    cluster_count = source_emb.shape[2]
    row_mask = (jnp.arange(row_count, dtype=jnp.int32) < valid_rows[0]).astype(jnp.float32)
    masked = (state.astype(jnp.float32) * row_mask).astype(jnp.bfloat16)
    hop_one = diffuse(masked, adj_tiles, adj_cols, row_mask)
    hop_two = diffuse(hop_one, adj_tiles, adj_cols, row_mask)
    member = (cluster_of[:, None] == jnp.arange(cluster_count, dtype=jnp.int32)[None, :]).astype(
        jnp.bfloat16
    )
    cluster_sums = jnp.dot(masked, member, preferred_element_type=jnp.float32)
    counts = jnp.dot(
        row_mask.astype(jnp.bfloat16)[None, :], member, preferred_element_type=jnp.float32
    )
    cluster_sums, counts = (
        lax.psum(cluster_sums.astype(jnp.bfloat16), "dom").astype(jnp.float32),
        lax.psum(counts.astype(jnp.bfloat16), "dom").astype(jnp.float32),
    )
    pooled = cluster_sums / jnp.maximum(counts, 1.0)
    all_values = project(pooled, w_value)
    attended = attend(source_emb, target_emb, all_values)
    coarse_attn = (pooled + attended.reshape(channels, cluster_count)).astype(jnp.bfloat16)
    tile_size = coarse_tiles.shape[2]
    coarse_grid = coarse_attn.reshape(channels, cluster_count // tile_size, tile_size)
    picked = coarse_grid[:, coarse_cols]
    coarse_terms = jnp.einsum(
        "hnkj,nkji->hni", picked, coarse_tiles, preferred_element_type=jnp.float32
    )
    coarse = (
        coarse_attn.astype(jnp.float32) + coarse_terms.reshape(channels, cluster_count)
    ).astype(jnp.bfloat16)
    unpooled = jnp.take(coarse, cluster_of, axis=1)
    features = jnp.stack([masked, hop_one, hop_two, unpooled])
    gate_sums = jnp.einsum(
        "ghkc,kcr->ghr",
        w_gates,
        lax.all_gather(features, "feat", axis=1, tiled=True),
        preferred_element_type=jnp.float32,
    )
    input_terms = (
        jnp.einsum("ghf,fr->ghr", w_input, inputs, preferred_element_type=jnp.float32)
        + bias[:, :, None]
    )
    update = jax.nn.sigmoid(input_terms[0] + gate_sums[0])
    reset = jax.nn.sigmoid(input_terms[1] + gate_sums[1])
    candidate = jnp.tanh(input_terms[2] + reset * gate_sums[2])
    fresh_state = (update * masked.astype(jnp.float32) + (1.0 - update) * candidate) * row_mask
    return fresh_state.astype(jnp.bfloat16)


def solution(mesh):
    return jax.shard_map(
        body,
        mesh=mesh,
        in_specs=(
            P("feat", "dom"),
            P(None, "dom"),
            P("dom", None, None, None),
            P("dom", None),
            P("dom"),
            P("dom"),
            P(None, "feat", None, None),
            P(None, "feat", None),
            P(None, "feat"),
            P("feat", None, None),
            P("feat", None, None),
            P("feat", None, None),
            P(),
            P(),
        ),
        out_specs=P("feat", "dom"),
        check_vma=False,
    )
```

profile of v0, /device:TPU:1, one launch (start us, length us, event | category | flops | bytes accessed | tf_op | source)
XLA Modules:
  0.0 465.0 jit_solution(15305916377223197281)
XLA Ops:
  8.4 8.4 %fusion.15 = bf16[64,4096]{1,0:T(8,128)(2,1)} fusion(bf16[64,2048]{1,0:T(8,128)(2,1)S(1)} %multiply_convert_fusion.2, s32[2048]{0:T(1024)} %param.21), kind=kOutput, calls=%fused_computation.25 | convolution fusion | flops 1082392576 | bytes 794624 | tf_op jit(solution)/shard_map/dot_general | solution.py:85
  21.8 6.0 %fusion.9 = f32[1,4096]{1,0:T(1,128)S(1)} fusion(bf16[2048,1]{0,1:T(2,128)(2,1)S(1)} %reshape.241, s32[2048]{0:T(1024)S(1)} %copy-done.7), kind=kOutput, calls=%fused_computation.19 | convolution fusion | flops 25165824 | bytes 28672 | tf_op jit(solution)/shard_map/dot_general | solution.py:86
  27.9 67.7 %psum.15 = bf16[1,4096]{1,0:T(2,128)(2,1)S(1)} all-reduce(bf16[1,4096]{1,0:T(2,128)(2,1)S(1)} %convert_element_type.97), channel_id=1, replica_groups=mesh['dom'=16,'feat'=8] {'dom'}, use_global_device_ids=true, to_apply=%region_1.0 | all-reduce | flops 4096 | bytes 16384 | tf_op jit(solution)/shard_map/psum | solution.py:91
  97.8 1.7 fusion.47
  100.3 5.9 %collective-permute-start.3 = (bf16[64,128]{1,0:T(8,128)(2,1)S(1)}, bf16[64,128]{1,0:T(8,128)(2,1)S(1)}, u32[]{:S(2)}, u32[]{:S(2)}) collective-permute-start(bf16[64,128]{1,0:T(8,128)(2,1)S(1)} %get-tuple-element.51), channel_id=1, source_target_pairs={{8,0},{16,8},{24,16},{32,24},{40,32},{48,40},{56,48},{64,56},{72,6... | collective-permute-start | bytes 49160 | tf_op jit(solution)/shard_map/ppermute | solution.py:16
  111.3 1.7 convolution_bitcast_fusion.1
  114.1 1.9 reshape.187
  116.1 1.9 multiply_convert_fusion.1
  118.0 41.8 %all-reduce.2.cloned.1.call-done = bf16[64,4096]{1,0:T(8,128)(2,1)} async-done(((bf16[64,4096]{1,0:T(8,128)(2,1)}), bf16[64,4096]{1,0:T(8,128)(2,1)}) %all-reduce.2.cloned.1.call-update) | async-done | bytes 524304 | tf_op jit(solution)/shard_map/psum | solution.py:90
  159.8 2.6 fusion.16
  162.4 100.1 %while.10 = (s32[]{:T(128)}, f32[8,1,64,512]{3,2,1,0:T(8,128)}, f32[8,1,10,512]{3,0,1,2:T(8,128)}, f32[1,10,4096]{2,0,1:T(1,128)S(1)}, bf16[1,64,4096]{2,1,0:T(8,128)(2,1)}, /*index=5*/s32[]{:T(128)}) while((s32[]{:T(128)}, f32[8,1,64,512]{3,2,1,0:T(8,128)}, f32[8,1,10,512]{3,0,1,2:T(8,128)}, f32[1,10,4096]{2,0,1:T(1,128)S(1)}, ...), condition=%wide.region_5.6_spmd, body=%wide.region_2.5_spmd.sunk | while | flops 538967040 | bytes 28153968 | solution.py:55
  163.4 7.2 %maximum_reduce_fusion.2 = (f32[512]{0:T(512)S(1)}, f32[512,4096]{1,0:T(8,128)S(1)}) fusion(f32[1,10,4096]{2,0,1:T(1,128)S(1)} %get-tuple-element.108, f32[1,1,10,512]{3,0,1,2:T(1,128)S(1)} %constant_dynamic-slice_fusion.2), kind=kOutput, calls=%fused_computation.6.clone.1 | convolution fusion | flops 255852032 | bytes 8574976 | tf_op jit(solution)/shard_map/while/body/eval_jaxpr/hei,hej->hij/dot_general | solution.py:46
  172.1 2.9 fusion.65
  175.9 7.2 %maximum_reduce_fusion.2 = (f32[512]{0:T(512)S(1)}, f32[512,4096]{1,0:T(8,128)S(1)}) fusion(f32[1,10,4096]{2,0,1:T(1,128)S(1)} %get-tuple-element.108, f32[1,1,10,512]{3,0,1,2:T(1,128)S(1)} %constant_dynamic-slice_fusion.2), kind=kOutput, calls=%fused_computation.6.clone.1 | convolution fusion | flops 255852032 | bytes 8574976 | tf_op jit(solution)/shard_map/while/body/eval_jaxpr/hei,hej->hij/dot_general | solution.py:46
  184.6 2.9 fusion.65
  188.4 7.2 %maximum_reduce_fusion.2 = (f32[512]{0:T(512)S(1)}, f32[512,4096]{1,0:T(8,128)S(1)}) fusion(f32[1,10,4096]{2,0,1:T(1,128)S(1)} %get-tuple-element.108, f32[1,1,10,512]{3,0,1,2:T(1,128)S(1)} %constant_dynamic-slice_fusion.2), kind=kOutput, calls=%fused_computation.6.clone.1 | convolution fusion | flops 255852032 | bytes 8574976 | tf_op jit(solution)/shard_map/while/body/eval_jaxpr/hei,hej->hij/dot_general | solution.py:46
  197.1 2.9 fusion.65
  200.9 7.2 %maximum_reduce_fusion.2 = (f32[512]{0:T(512)S(1)}, f32[512,4096]{1,0:T(8,128)S(1)}) fusion(f32[1,10,4096]{2,0,1:T(1,128)S(1)} %get-tuple-element.108, f32[1,1,10,512]{3,0,1,2:T(1,128)S(1)} %constant_dynamic-slice_fusion.2), kind=kOutput, calls=%fused_computation.6.clone.1 | convolution fusion | flops 255852032 | bytes 8574976 | tf_op jit(solution)/shard_map/while/body/eval_jaxpr/hei,hej->hij/dot_general | solution.py:46
  209.6 2.9 fusion.65
  213.4 7.2 %maximum_reduce_fusion.2 = (f32[512]{0:T(512)S(1)}, f32[512,4096]{1,0:T(8,128)S(1)}) fusion(f32[1,10,4096]{2,0,1:T(1,128)S(1)} %get-tuple-element.108, f32[1,1,10,512]{3,0,1,2:T(1,128)S(1)} %constant_dynamic-slice_fusion.2), kind=kOutput, calls=%fused_computation.6.clone.1 | convolution fusion | flops 255852032 | bytes 8574976 | tf_op jit(solution)/shard_map/while/body/eval_jaxpr/hei,hej->hij/dot_general | solution.py:46
  222.1 2.9 fusion.65
  225.9 7.2 %maximum_reduce_fusion.2 = (f32[512]{0:T(512)S(1)}, f32[512,4096]{1,0:T(8,128)S(1)}) fusion(f32[1,10,4096]{2,0,1:T(1,128)S(1)} %get-tuple-element.108, f32[1,1,10,512]{3,0,1,2:T(1,128)S(1)} %constant_dynamic-slice_fusion.2), kind=kOutput, calls=%fused_computation.6.clone.1 | convolution fusion | flops 255852032 | bytes 8574976 | tf_op jit(solution)/shard_map/while/body/eval_jaxpr/hei,hej->hij/dot_general | solution.py:46
  234.6 2.9 fusion.65
  238.4 7.2 %maximum_reduce_fusion.2 = (f32[512]{0:T(512)S(1)}, f32[512,4096]{1,0:T(8,128)S(1)}) fusion(f32[1,10,4096]{2,0,1:T(1,128)S(1)} %get-tuple-element.108, f32[1,1,10,512]{3,0,1,2:T(1,128)S(1)} %constant_dynamic-slice_fusion.2), kind=kOutput, calls=%fused_computation.6.clone.1 | convolution fusion | flops 255852032 | bytes 8574976 | tf_op jit(solution)/shard_map/while/body/eval_jaxpr/hei,hej->hij/dot_general | solution.py:46
  247.1 2.9 fusion.65
  250.9 7.2 %maximum_reduce_fusion.2 = (f32[512]{0:T(512)S(1)}, f32[512,4096]{1,0:T(8,128)S(1)}) fusion(f32[1,10,4096]{2,0,1:T(1,128)S(1)} %get-tuple-element.108, f32[1,1,10,512]{3,0,1,2:T(1,128)S(1)} %constant_dynamic-slice_fusion.2), kind=kOutput, calls=%fused_computation.6.clone.1 | convolution fusion | flops 255852032 | bytes 8574976 | tf_op jit(solution)/shard_map/while/body/eval_jaxpr/hei,hej->hij/dot_general | solution.py:46
  259.6 2.9 fusion.65
  265.8 2.4 convolution_bitcast_fusion
  270.6 8.0 %gather_fusion.3 = bf16[2048,64]{1,0:T(8,128)(2,1)} fusion(bf16[64,4096]{0,1:T(8,128)(2,1)S(1)} %copy.39, s32[2048]{0:T(1024)S(1)} %fusion.43), kind=kCustom, calls=%fused_computation.3 | custom fusion | bytes 532480 | tf_op jit(solution)/shard_map/jit(_take)/gather | solution.py:106
  279.9 2.2 pad_maximum_fusion
  283.8 167.9 %all-gather.2.cloned.1.call-done = bf16[4,512,2048]{2,1,0:T(8,128)(2,1)} async-done(((bf16[4,64,2048]{2,1,0:T(8,128)(2,1)}), bf16[4,512,2048]{2,1,0:T(8,128)(2,1)}) %all-gather.2.cloned.1.call-update) | async-done | bytes 8388624 | tf_op jit(solution)/shard_map/all_gather | solution.py:111
  451.7 5.4 %fusion.17 = f32[3,64,2048]{2,1,0:T(8,128)S(1)} fusion(bf16[4,512,2048]{2,1,0:T(8,128)(2,1)} %all-gather.2.cloned.1.call-done, bf16[3,64,4,512]{3,2,1,0:T(4,128)(2,1)} %param.22), kind=kOutput, calls=%fused_computation.28 | convolution fusion | flops 1610612736 | bytes 10747904 | tf_op jit(solution)/shard_map/ghkc,kcr->ghr/dot_general | solution.py:108
  (112 shorter events, 44.3 us)
Async XLA Ops:
  6.5 91.3 %copy-start = (bf16[16,4,128,128]{3,2,1,0:T(8,128)(2,1)S(1)}, bf16[16,4,128,128]{3,2,1,0:T(8,128)(2,1)}, u32[]{:S(2)}) copy-start(bf16[16,4,128,128]{3,2,1,0:T(8,128)(2,1)} %param.18) | copy-start | bytes 6291460
  6.5 13.3 %copy-start.3 = (bf16[64,2048]{1,0:T(8,128)(2,1)S(1)}, bf16[64,2048]{1,0:T(8,128)(2,1)}, u32[]{:S(2)}) copy-start(bf16[64,2048]{1,0:T(8,128)(2,1)} %param.16) | copy-start | bytes 786436
  6.5 13.3 %copy-start.7 = (s32[2048]{0:T(1024)S(1)}, s32[2048]{0:T(1024)}, u32[]{:S(2)}) copy-start(s32[2048]{0:T(1024)} %param.21) | copy-start | bytes 24580
  6.5 14.0 %copy-start.6 = (f32[1,10,4096]{2,0,1:T(1,128)S(1)}, f32[1,10,4096]{2,0,1:T(1,128)}, u32[]{:S(2)}) copy-start(f32[1,10,4096]{2,0,1:T(1,128)} %param.26) | copy-start | bytes 491524
  6.5 153.2 %all-reduce.2.cloned.1.call-start = ((), (), s32[]{:S(2)}) async-start(), calls=%async_computation | async-start | bytes 1048576 | tf_op jit(solution)/shard_map/psum | solution.py:90
  16.8 78.9 %copy-start.12 = (s32[32,2]{0,1:T(2,128)S(1)}, s32[32,2]{0,1:T(2,128)}, u32[]{:S(2)}) copy-start(s32[32,2]{0,1:T(2,128)} %param.29) | copy-start | bytes 772
  16.8 78.9 %copy-start.10 = (s32[16,4]{0,1:T(4,128)S(1)}, s32[16,4]{0,1:T(4,128)}, u32[]{:S(2)}) copy-start(s32[16,4]{0,1:T(4,128)} %param.19) | copy-start | bytes 772
  16.8 434.9 %all-gather.2.cloned.1.call-start = ((), (), s32[]{:S(2)}) async-start(), calls=%async_computation.1 | async-start | bytes 9437184 | tf_op jit(solution)/shard_map/all_gather | solution.py:111
  16.9 79.2 %collective-permute-start.1 = (bf16[64,128]{1,0:T(8,128)(2,1)S(1)}, bf16[64,128]{1,0:T(8,128)(2,1)S(1)}, u32[]{:S(2)}, u32[]{:S(2)}) collective-permute-start(bf16[64,128]{1,0:T(8,128)(2,1)S(1)} %get-tuple-element.53), channel_id=1, source_target_pairs={{8,0},{16,8},{24,16},{32,24},{40,32},{48,40},{56,48},{64,56},{72,6... | collective-permute-start | bytes 49160 | tf_op jit(solution)/shard_map/ppermute | solution.py:16
  18.3 77.7 %collective-permute-start = (bf16[64,128]{1,0:T(8,128)(2,1)S(1)}, bf16[64,128]{1,0:T(8,128)(2,1)S(1)}, u32[]{:S(2)}, u32[]{:S(2)}) collective-permute-start(bf16[64,128]{1,0:T(8,128)(2,1)S(1)} %get-tuple-element.52), channel_id=1, source_target_pairs={{0,8},{8,16},{16,24},{24,32},{32,40},{40,48},{48,56},{56,64},{64,7... | collective-permute-start | bytes 49160 | tf_op jit(solution)/shard_map/ppermute | solution.py:15
  97.8 62.0 %copy-start.13 = (bf16[1,64,64]{2,1,0:T(8,128)(2,1)S(1)}, bf16[1,64,64]{2,1,0:T(8,128)(2,1)}, u32[]{:S(2)}) copy-start(bf16[1,64,64]{2,1,0:T(8,128)(2,1)} %param.25) | copy-start | bytes 24580
  99.6 62.9 %copy-start.1 = (f32[1,10,4096]{2,0,1:T(1,128)S(1)}, f32[1,10,4096]{2,0,1:T(1,128)}, u32[]{:S(2)}) copy-start(f32[1,10,4096]{2,0,1:T(1,128)} %param.27) | copy-start | bytes 491524
  99.6 0.7 copy-start.4
  100.3 8.2 %collective-permute-start.3 = (bf16[64,128]{1,0:T(8,128)(2,1)S(1)}, bf16[64,128]{1,0:T(8,128)(2,1)S(1)}, u32[]{:S(2)}, u32[]{:S(2)}) collective-permute-start(bf16[64,128]{1,0:T(8,128)(2,1)S(1)} %get-tuple-element.51), channel_id=1, source_target_pairs={{8,0},{16,8},{24,16},{32,24},{40,32},{48,40},{56,48},{64,56},{72,6... | collective-permute-start | bytes 49160 | tf_op jit(solution)/shard_map/ppermute | solution.py:16
  106.3 2.3 collective-permute-start.2
  162.4 101.4 %copy-start.5 = (bf16[64,4096]{1,0:T(8,128)(2,1)S(1)}, bf16[64,4096]{1,0:T(8,128)(2,1)}, u32[]{:S(2)}) copy-start(bf16[64,4096]{1,0:T(8,128)(2,1)} %all-reduce.2.cloned.1.call-done) | copy-start | bytes 1572868
  163.4 8.7 %copy-start.14 = (bf16[1,64,4096]{2,1,0:T(8,128)(2,1)S(1)}, bf16[1,64,4096]{2,1,0:T(8,128)(2,1)}, u32[]{:S(2)}) copy-start(bf16[1,64,4096]{2,1,0:T(8,128)(2,1)} %get-tuple-element.109) | copy-start | bytes 1572868 | tf_op jit(solution)/shard_map/while
  175.9 8.7 %copy-start.14 = (bf16[1,64,4096]{2,1,0:T(8,128)(2,1)S(1)}, bf16[1,64,4096]{2,1,0:T(8,128)(2,1)}, u32[]{:S(2)}) copy-start(bf16[1,64,4096]{2,1,0:T(8,128)(2,1)} %get-tuple-element.109) | copy-start | bytes 1572868 | tf_op jit(solution)/shard_map/while
  188.4 8.7 %copy-start.14 = (bf16[1,64,4096]{2,1,0:T(8,128)(2,1)S(1)}, bf16[1,64,4096]{2,1,0:T(8,128)(2,1)}, u32[]{:S(2)}) copy-start(bf16[1,64,4096]{2,1,0:T(8,128)(2,1)} %get-tuple-element.109) | copy-start | bytes 1572868 | tf_op jit(solution)/shard_map/while
  200.9 8.7 %copy-start.14 = (bf16[1,64,4096]{2,1,0:T(8,128)(2,1)S(1)}, bf16[1,64,4096]{2,1,0:T(8,128)(2,1)}, u32[]{:S(2)}) copy-start(bf16[1,64,4096]{2,1,0:T(8,128)(2,1)} %get-tuple-element.109) | copy-start | bytes 1572868 | tf_op jit(solution)/shard_map/while
  213.4 8.7 %copy-start.14 = (bf16[1,64,4096]{2,1,0:T(8,128)(2,1)S(1)}, bf16[1,64,4096]{2,1,0:T(8,128)(2,1)}, u32[]{:S(2)}) copy-start(bf16[1,64,4096]{2,1,0:T(8,128)(2,1)} %get-tuple-element.109) | copy-start | bytes 1572868 | tf_op jit(solution)/shard_map/while
  225.9 8.7 %copy-start.14 = (bf16[1,64,4096]{2,1,0:T(8,128)(2,1)S(1)}, bf16[1,64,4096]{2,1,0:T(8,128)(2,1)}, u32[]{:S(2)}) copy-start(bf16[1,64,4096]{2,1,0:T(8,128)(2,1)} %get-tuple-element.109) | copy-start | bytes 1572868 | tf_op jit(solution)/shard_map/while
  238.4 8.7 %copy-start.14 = (bf16[1,64,4096]{2,1,0:T(8,128)(2,1)S(1)}, bf16[1,64,4096]{2,1,0:T(8,128)(2,1)}, u32[]{:S(2)}) copy-start(bf16[1,64,4096]{2,1,0:T(8,128)(2,1)} %get-tuple-element.109) | copy-start | bytes 1572868 | tf_op jit(solution)/shard_map/while
  250.9 8.7 %copy-start.14 = (bf16[1,64,4096]{2,1,0:T(8,128)(2,1)S(1)}, bf16[1,64,4096]{2,1,0:T(8,128)(2,1)}, u32[]{:S(2)}) copy-start(bf16[1,64,4096]{2,1,0:T(8,128)(2,1)} %get-tuple-element.109) | copy-start | bytes 1572868 | tf_op jit(solution)/shard_map/while
  264.1 18.0 %copy-start.8 = (bf16[2,2048]{1,0:T(2,128)(2,1)S(1)}, bf16[2,2048]{1,0:T(2,128)(2,1)}, u32[]{:S(2)}) copy-start(bf16[2,2048]{1,0:T(2,128)(2,1)} %param.17) | copy-start | bytes 24580
  264.1 18.0 %copy-start.9 = (f32[3,64]{1,0:T(4,128)S(1)}, f32[3,64]{1,0:T(4,128)}, u32[]{:S(2)}) copy-start(f32[3,64]{1,0:T(4,128)} %param.24) | copy-start | bytes 2308
  264.1 18.0 %copy-start.11 = (bf16[3,64,2]{1,2,0:T(2,128)(2,1)S(1)}, bf16[3,64,2]{1,2,0:T(2,128)(2,1)}, u32[]{:S(2)}) copy-start(bf16[3,64,2]{1,2,0:T(2,128)(2,1)} %param.23) | copy-start | bytes 2308
  451.7 5.4 %copy-start.2 = (f32[3,64,2048]{2,1,0:T(8,128)S(1)}, f32[3,64,2048]{2,1,0:T(8,128)}, u32[]{:S(2)}) copy-start(f32[3,64,2048]{2,1,0:T(8,128)} %convolution_add_fusion) | copy-start | bytes 4718596
Sparse Core Ops, SparseCore 0:
  16.9 142.7 all-reduce.1
  282.3 169.3 all-gather.1
where the time goes:
time: 466 us; the launch traced here: 465 us
  waiting for transfers between devices  210 us (45%)
  matrix products  110 us (24%)
  blocking collectives  67.7 us (15%)
  local copies, waits for them, and re-layouts  32 us (7%)
  other arithmetic  21.6 us (5%)
  between operations  14.5 us (3%)
  starting transfers between devices  8.94 us (2%)
    all_gather x1, waiting for transfers between devices, body(): lax.all_gather(features, 'feat', axis=1, tiled=True)  168 us
    psum x1, blocking collectives, body(): lax.psum(counts.astype(jnp.bfloat16), 'dom').astype(jnp.float32)  67.7 us
    dot_general x8, matrix products, one_block(): jnp.einsum('hei,hej->hij', source_block, target_emb, precision=lax.Precis...  57.3 us
    psum x1, waiting for transfers between devices, body(): lax.psum(cluster_sums.astype(jnp.bfloat16), 'dom').astype(jnp.float32)  41.8 us
    dot_general x8, matrix products, one_block(): jnp.einsum('hdj,hij->hdi', values, weights, preferred_element_type=jnp.fl...  23.1 us
    reduce_sum x8, other arithmetic, one_block(): jnp.sum(raised, axis=2, keepdims=True)  12 us
  transfers between devices with their start and end apart: 6, of which 2 were waited for; matrix products, arithmetic and copies ran while one was open for 5% of the time, Pallas kernels for 0%

commit v1 on v0

--- a/solution.py
+++ b/solution.py
@@ -108,7 +108,9 @@
     gate_sums = jnp.einsum(
         "ghkc,kcr->ghr",
         w_gates,
-        lax.all_gather(features, "feat", axis=1, tiled=True),
+        jnp.concatenate(
+            lax.all_to_all(jnp.stack([features] * lax.axis_size("feat")), "feat", 0, 0), axis=1
+        ),
         preferred_element_type=jnp.float32,
     )
     input_terms = (

time: 466 us -> 410 us (0.88)
  waiting for transfers between devices: 210 us -> 142 us
  local copies, waits for them, and re-layouts: 32 us -> 44 us
  starting transfers between devices: 8.94 us -> 14.1 us
    all_gather x1 -> x0, waiting for transfers between devices: 168 us -> none  [body(): lax.all_gather(features, 'feat', axis=1, tiled=True)]
    all_to_all x0 -> x1, waiting for transfers between devices: none -> 91.8 us  [body(): lax.all_to_all(jnp.stack([features] * lax.axis_size('feat')), 'feat', 0, 0)]
    reshape x0 -> x1, local copies, waits for them, and re-layouts: none -> 8.36 us  [body(): jnp.concatenate(lax.all_to_all(jnp.stack([features] * lax.axis_size('feat...]
    psum x1, waiting for transfers between devices: 41.8 us -> 49.8 us  [body(): lax.psum(cluster_sums.astype(jnp.bfloat16), 'dom').astype(jnp.float32)]
    all_to_all x0 -> x1, starting transfers between devices: none -> 5.3 us  [body(): lax.all_to_all(jnp.stack([features] * lax.axis_size('feat')), 'feat', 0, 0)]
  transfers between devices with their start and end apart: 6 -> 6, of which waited for: 2 -> 2; matrix products, arithmetic and copies ran while one was open for 5% -> 8% of each run, Pallas kernels for 0% -> 0%
where the time goes in v1:
time: 410 us; the launch traced here: 409 us
  waiting for transfers between devices  142 us (35%)
  matrix products  110 us (27%)
  blocking collectives  63.5 us (15%)
  local copies, waits for them, and re-layouts  44 us (11%)
  other arithmetic  20.7 us (5%)
  between operations  14.5 us (4%)
  starting transfers between devices  14.1 us (3%)
    all_to_all x1, waiting for transfers between devices, body(): lax.all_to_all(jnp.stack([features] * lax.axis_size('feat')), 'feat', 0, 0)  91.8 us
    psum x1, blocking collectives, body(): lax.psum(counts.astype(jnp.bfloat16), 'dom').astype(jnp.float32)  63.5 us
    dot_general x8, matrix products, one_block(): jnp.einsum('hei,hej->hij', source_block, target_emb, precision=lax.Precis...  57.3 us
    psum x1, waiting for transfers between devices, body(): lax.psum(cluster_sums.astype(jnp.bfloat16), 'dom').astype(jnp.float32)  49.8 us
    dot_general x8, matrix products, one_block(): jnp.einsum('hdj,hij->hdi', values, weights, preferred_element_type=jnp.fl...  23.1 us
    reduce_sum x8, other arithmetic, one_block(): jnp.sum(raised, axis=2, keepdims=True)  12 us
    gather x2, local copies, waits for them, and re-layouts, body(): unpooled = jnp.take(coarse, cluster_of, axis=1)  9.23 us
    dot_general x1, matrix products, body(): cluster_sums = jnp.dot(masked, member, preferred_element_type=jnp.float32)  8.42 us
  transfers between devices with their start and end apart: 6, of which 2 were waited for; matrix products, arithmetic and copies ran while one was open for 8% of the time, Pallas kernels for 0%

profile of v1, /device:TPU:1, one launch (start us, length us, event | category | flops | bytes accessed | tf_op | source)
XLA Modules:
  0.0 408.8 jit_solution(9012399938136680418)
XLA Ops:
  8.4 2.7 collective-permute-start
  11.1 8.4 %fusion.13 = bf16[64,4096]{1,0:T(8,128)(2,1)} fusion(bf16[64,2048]{1,0:T(8,128)(2,1)S(1)} %multiply_convert_fusion.2, s32[2048]{0:T(1024)} %param.21), kind=kOutput, calls=%fused_computation.23 | convolution fusion | flops 1082392576 | bytes 794624 | tf_op jit(solution)/shard_map/dot_general | solution.py:85
  20.5 6.2 %fusion.9 = f32[1,4096]{1,0:T(1,128)S(1)} fusion(bf16[2048,1]{0,1:T(2,128)(2,1)S(1)} %reshape.251, s32[2048]{0:T(1024)S(1)} %copy-done.7), kind=kOutput, calls=%fused_computation.19 | convolution fusion | flops 25165824 | bytes 28672 | tf_op jit(solution)/shard_map/dot_general | solution.py:86
  26.7 63.5 %psum.15 = bf16[1,4096]{1,0:T(2,128)(2,1)S(1)} all-reduce(bf16[1,4096]{1,0:T(2,128)(2,1)S(1)} %convert_element_type.97), channel_id=1, replica_groups=mesh['dom'=16,'feat'=8] {'dom'}, use_global_device_ids=true, to_apply=%region_1.0 | all-reduce | flops 4096 | bytes 16384 | tf_op jit(solution)/shard_map/psum | solution.py:91
  97.0 4.3 %collective-permute-start.3 = (bf16[64,128]{1,0:T(8,128)(2,1)S(1)}, bf16[64,128]{1,0:T(8,128)(2,1)S(1)}, u32[]{:S(2)}, u32[]{:S(2)}) collective-permute-start(bf16[64,128]{1,0:T(8,128)(2,1)S(1)} %get-tuple-element.56), channel_id=1, source_target_pairs={{8,0},{16,8},{24,16},{32,24},{40,32},{48,40},{56,48},{64,56},{72,6... | collective-permute-start | bytes 49160 | tf_op jit(solution)/shard_map/ppermute | solution.py:16
  109.2 1.9 reshape.195
  113.0 49.8 %all-reduce.2.cloned.1.call-done = bf16[64,4096]{1,0:T(8,128)(2,1)} async-done(((bf16[64,4096]{1,0:T(8,128)(2,1)}), bf16[64,4096]{1,0:T(8,128)(2,1)}) %all-reduce.2.cloned.1.call-update) | async-done | bytes 524304 | tf_op jit(solution)/shard_map/psum | solution.py:90
  162.8 2.6 fusion.14
  165.4 100.1 %while.10 = (s32[]{:T(128)}, f32[8,1,64,512]{3,2,1,0:T(8,128)}, f32[8,1,10,512]{3,0,1,2:T(8,128)}, f32[1,10,4096]{2,0,1:T(1,128)S(1)}, bf16[1,64,4096]{2,1,0:T(8,128)(2,1)}, /*index=5*/s32[]{:T(128)}) while((s32[]{:T(128)}, f32[8,1,64,512]{3,2,1,0:T(8,128)}, f32[8,1,10,512]{3,0,1,2:T(8,128)}, f32[1,10,4096]{2,0,1:T(1,128)S(1)}, ...), condition=%wide.region_5.6_spmd, body=%wide.region_2.5_spmd.sunk | while | flops 538967040 | bytes 28154468 | solution.py:55
  166.5 7.2 %maximum_reduce_fusion.2 = (f32[512]{0:T(512)S(1)}, f32[512,4096]{1,0:T(8,128)S(1)}) fusion(f32[1,10,4096]{2,0,1:T(1,128)S(1)} %get-tuple-element.113, f32[1,1,10,512]{3,0,1,2:T(1,128)S(1)} %constant_dynamic-slice_fusion.2), kind=kOutput, calls=%fused_computation.6.clone.1 | convolution fusion | flops 255852032 | bytes 8574976 | tf_op jit(solution)/shard_map/while/body/eval_jaxpr/hei,hej->hij/dot_general | solution.py:46
  175.1 2.9 fusion.61
  179.0 7.2 %maximum_reduce_fusion.2 = (f32[512]{0:T(512)S(1)}, f32[512,4096]{1,0:T(8,128)S(1)}) fusion(f32[1,10,4096]{2,0,1:T(1,128)S(1)} %get-tuple-element.113, f32[1,1,10,512]{3,0,1,2:T(1,128)S(1)} %constant_dynamic-slice_fusion.2), kind=kOutput, calls=%fused_computation.6.clone.1 | convolution fusion | flops 255852032 | bytes 8574976 | tf_op jit(solution)/shard_map/while/body/eval_jaxpr/hei,hej->hij/dot_general | solution.py:46
  187.6 2.9 fusion.61
  191.5 7.2 %maximum_reduce_fusion.2 = (f32[512]{0:T(512)S(1)}, f32[512,4096]{1,0:T(8,128)S(1)}) fusion(f32[1,10,4096]{2,0,1:T(1,128)S(1)} %get-tuple-element.113, f32[1,1,10,512]{3,0,1,2:T(1,128)S(1)} %constant_dynamic-slice_fusion.2), kind=kOutput, calls=%fused_computation.6.clone.1 | convolution fusion | flops 255852032 | bytes 8574976 | tf_op jit(solution)/shard_map/while/body/eval_jaxpr/hei,hej->hij/dot_general | solution.py:46
  200.1 2.9 fusion.61
  204.0 7.2 %maximum_reduce_fusion.2 = (f32[512]{0:T(512)S(1)}, f32[512,4096]{1,0:T(8,128)S(1)}) fusion(f32[1,10,4096]{2,0,1:T(1,128)S(1)} %get-tuple-element.113, f32[1,1,10,512]{3,0,1,2:T(1,128)S(1)} %constant_dynamic-slice_fusion.2), kind=kOutput, calls=%fused_computation.6.clone.1 | convolution fusion | flops 255852032 | bytes 8574976 | tf_op jit(solution)/shard_map/while/body/eval_jaxpr/hei,hej->hij/dot_general | solution.py:46
  212.6 2.9 fusion.61
  216.5 7.2 %maximum_reduce_fusion.2 = (f32[512]{0:T(512)S(1)}, f32[512,4096]{1,0:T(8,128)S(1)}) fusion(f32[1,10,4096]{2,0,1:T(1,128)S(1)} %get-tuple-element.113, f32[1,1,10,512]{3,0,1,2:T(1,128)S(1)} %constant_dynamic-slice_fusion.2), kind=kOutput, calls=%fused_computation.6.clone.1 | convolution fusion | flops 255852032 | bytes 8574976 | tf_op jit(solution)/shard_map/while/body/eval_jaxpr/hei,hej->hij/dot_general | solution.py:46
  225.1 2.9 fusion.61
  229.0 7.2 %maximum_reduce_fusion.2 = (f32[512]{0:T(512)S(1)}, f32[512,4096]{1,0:T(8,128)S(1)}) fusion(f32[1,10,4096]{2,0,1:T(1,128)S(1)} %get-tuple-element.113, f32[1,1,10,512]{3,0,1,2:T(1,128)S(1)} %constant_dynamic-slice_fusion.2), kind=kOutput, calls=%fused_computation.6.clone.1 | convolution fusion | flops 255852032 | bytes 8574976 | tf_op jit(solution)/shard_map/while/body/eval_jaxpr/hei,hej->hij/dot_general | solution.py:46
  237.6 2.9 fusion.61
  241.5 7.2 %maximum_reduce_fusion.2 = (f32[512]{0:T(512)S(1)}, f32[512,4096]{1,0:T(8,128)S(1)}) fusion(f32[1,10,4096]{2,0,1:T(1,128)S(1)} %get-tuple-element.113, f32[1,1,10,512]{3,0,1,2:T(1,128)S(1)} %constant_dynamic-slice_fusion.2), kind=kOutput, calls=%fused_computation.6.clone.1 | convolution fusion | flops 255852032 | bytes 8574976 | tf_op jit(solution)/shard_map/while/body/eval_jaxpr/hei,hej->hij/dot_general | solution.py:46
  250.1 2.9 fusion.61
  254.0 7.2 %maximum_reduce_fusion.2 = (f32[512]{0:T(512)S(1)}, f32[512,4096]{1,0:T(8,128)S(1)}) fusion(f32[1,10,4096]{2,0,1:T(1,128)S(1)} %get-tuple-element.113, f32[1,1,10,512]{3,0,1,2:T(1,128)S(1)} %constant_dynamic-slice_fusion.2), kind=kOutput, calls=%fused_computation.6.clone.1 | convolution fusion | flops 255852032 | bytes 8574976 | tf_op jit(solution)/shard_map/while/body/eval_jaxpr/hei,hej->hij/dot_general | solution.py:46
  262.6 2.9 fusion.61
  268.8 2.4 convolution_bitcast_fusion.1
  273.6 8.0 %gather_fusion.3 = bf16[2048,64]{1,0:T(8,128)(2,1)} fusion(bf16[64,4096]{0,1:T(8,128)(2,1)S(1)} %copy.53, s32[2048]{0:T(1024)S(1)} %fusion.38), kind=kCustom, calls=%fused_computation.3 | custom fusion | bytes 532480 | tf_op jit(solution)/shard_map/jit(_take)/gather | solution.py:106
  284.1 4.3 %stack.8 = bf16[8,4,64,2048]{3,2,1,0:T(8,128)(2,1)} broadcast(bf16[4,64,2048]{2,1,0:T(8,128)(2,1)S(1)} %pad_maximum_fusion), dimensions={1,2,3} | broadcast | bytes 9437184 | tf_op jit(solution)/shard_map/stack | solution.py:112
  288.5 5.3 %all-to-all-start = ((bf16[8,4,64,2048]{3,2,1,0:T(8,128)(2,1)}), bf16[8,4,64,2048]{3,2,1,0:T(8,128)(2,1)}, u32[]{:S(2)}, u32[]{:S(2)}) async-start(bf16[8,4,64,2048]{3,2,1,0:T(8,128)(2,1)} %stack.8), calls=%async_computation | async-start | bytes 16777216 | tf_op jit(solution)/shard_map/all_to_all | solution.py:112
  295.4 91.8 %all-to-all-done = bf16[8,4,64,2048]{3,2,1,0:T(8,128)(2,1)} async-done(((bf16[8,4,64,2048]{3,2,1,0:T(8,128)(2,1)}), bf16[8,4,64,2048]{3,2,1,0:T(8,128)(2,1)}, u32[]{:S(2)}, u32[]{:S(2)}) %all-to-all-start) | async-done | bytes 8388640 | tf_op jit(solution)/shard_map/all_to_all | solution.py:112
  387.2 8.4 %copy.55 = bf16[4,8,64,2048]{3,2,1,0:T(8,128)(2,1)} copy(bf16[4,8,64,2048]{3,2,0,1:T(8,128)(2,1)} %bitcast.32) | data formatting | bytes 16777216 | tf_op jit(solution)/shard_map/reshape | solution.py:111
  395.5 5.3 %convolution_bitcast_fusion = f32[3,64,2048]{2,1,0:T(8,128)S(1)} fusion(bf16[4,512,2048,1]{2,1,0,3:T(8,128)(2,1)} %bitcast.144, bf16[3,64,4,512]{3,2,1,0:T(4,128)(2,1)S(1)} %copy-done.13), kind=kOutput, calls=%fused_computation.26 | convolution fusion | flops 1610612736 | bytes 10747904 | tf_op jit(solution)/shard_map/ghkc,kcr->ghr/dot_general | solution.py:108
  (115 shorter events, 48.9 us)
Async XLA Ops:
  6.5 86.9 %copy-start = (bf16[16,4,128,128]{3,2,1,0:T(8,128)(2,1)S(1)}, bf16[16,4,128,128]{3,2,1,0:T(8,128)(2,1)}, u32[]{:S(2)}) copy-start(bf16[16,4,128,128]{3,2,1,0:T(8,128)(2,1)} %param.18) | copy-start | bytes 6291460
  6.5 13.0 %copy-start.3 = (bf16[64,2048]{1,0:T(8,128)(2,1)S(1)}, bf16[64,2048]{1,0:T(8,128)(2,1)}, u32[]{:S(2)}) copy-start(bf16[64,2048]{1,0:T(8,128)(2,1)} %param.16) | copy-start | bytes 786436
  6.5 13.0 %copy-start.7 = (s32[2048]{0:T(1024)S(1)}, s32[2048]{0:T(1024)}, u32[]{:S(2)}) copy-start(s32[2048]{0:T(1024)} %param.21) | copy-start | bytes 24580
  6.5 13.8 %copy-start.10 = (s32[16,4]{0,1:T(4,128)S(1)}, s32[16,4]{0,1:T(4,128)}, u32[]{:S(2)}) copy-start(s32[16,4]{0,1:T(4,128)} %param.19) | copy-start | bytes 772
  6.5 156.2 %all-reduce.2.cloned.1.call-start = ((), (), s32[]{:S(2)}) async-start(), calls=%async_computation.1 | async-start | bytes 1048576 | tf_op jit(solution)/shard_map/psum | solution.py:90
  8.4 83.3 %collective-permute-start = (bf16[64,128]{1,0:T(8,128)(2,1)S(1)}, bf16[64,128]{1,0:T(8,128)(2,1)S(1)}, u32[]{:S(2)}, u32[]{:S(2)}) collective-permute-start(bf16[64,128]{1,0:T(8,128)(2,1)S(1)} %get-tuple-element.57), channel_id=1, source_target_pairs={{0,8},{8,16},{16,24},{24,32},{32,40},{40,48},{48,56},{56,64},{64,7... | collective-permute-start | bytes 49160 | tf_op jit(solution)/shard_map/ppermute | solution.py:15
  11.1 79.2 %copy-start.6 = (f32[1,10,4096]{2,0,1:T(1,128)S(1)}, f32[1,10,4096]{2,0,1:T(1,128)}, u32[]{:S(2)}) copy-start(f32[1,10,4096]{2,0,1:T(1,128)} %param.26) | copy-start | bytes 491524
  11.1 80.6 %collective-permute-start.1 = (bf16[64,128]{1,0:T(8,128)(2,1)S(1)}, bf16[64,128]{1,0:T(8,128)(2,1)S(1)}, u32[]{:S(2)}, u32[]{:S(2)}) collective-permute-start(bf16[64,128]{1,0:T(8,128)(2,1)S(1)} %get-tuple-element.58), channel_id=1, source_target_pairs={{8,0},{16,8},{24,16},{32,24},{40,32},{48,40},{56,48},{64,56},{72,6... | collective-permute-start | bytes 49160 | tf_op jit(solution)/shard_map/ppermute | solution.py:16
  19.5 72.0 %copy-start.12 = (s32[32,2]{0,1:T(2,128)S(1)}, s32[32,2]{0,1:T(2,128)}, u32[]{:S(2)}) copy-start(s32[32,2]{0,1:T(2,128)} %param.29) | copy-start | bytes 772
  93.4 69.4 %copy-start.14 = (bf16[1,64,64]{2,1,0:T(8,128)(2,1)S(1)}, bf16[1,64,64]{2,1,0:T(8,128)(2,1)}, u32[]{:S(2)}) copy-start(bf16[1,64,64]{2,1,0:T(8,128)(2,1)} %param.25) | copy-start | bytes 24580
  95.2 70.3 %copy-start.1 = (f32[1,10,4096]{2,0,1:T(1,128)S(1)}, f32[1,10,4096]{2,0,1:T(1,128)}, u32[]{:S(2)}) copy-start(f32[1,10,4096]{2,0,1:T(1,128)} %param.27) | copy-start | bytes 491524
  95.2 6.1 %copy-start.4 = (bf16[64,2048]{1,0:T(8,128)(2,1)}, bf16[64,2048]{1,0:T(8,128)(2,1)S(1)}, u32[]{:S(2)}) copy-start(bf16[64,2048]{1,0:T(8,128)(2,1)S(1)} %fusion.17) | copy-start | bytes 786436
  95.3 8.3 %collective-permute-start.2 = (bf16[64,128]{1,0:T(8,128)(2,1)S(1)}, bf16[64,128]{1,0:T(8,128)(2,1)S(1)}, u32[]{:S(2)}, u32[]{:S(2)}) collective-permute-start(bf16[64,128]{1,0:T(8,128)(2,1)S(1)} %get-tuple-element.55), channel_id=1, source_target_pairs={{0,8},{8,16},{16,24},{24,32},{32,40},{40,48},{48,56},{56,64},{64,7... | collective-permute-start | bytes 49160 | tf_op jit(solution)/shard_map/ppermute | solution.py:15
  97.0 6.6 %collective-permute-start.3 = (bf16[64,128]{1,0:T(8,128)(2,1)S(1)}, bf16[64,128]{1,0:T(8,128)(2,1)S(1)}, u32[]{:S(2)}, u32[]{:S(2)}) collective-permute-start(bf16[64,128]{1,0:T(8,128)(2,1)S(1)} %get-tuple-element.56), channel_id=1, source_target_pairs={{8,0},{16,8},{24,16},{32,24},{40,32},{48,40},{56,48},{64,56},{72,6... | collective-permute-start | bytes 49160 | tf_op jit(solution)/shard_map/ppermute | solution.py:16
  165.4 101.4 %copy-start.5 = (bf16[64,4096]{1,0:T(8,128)(2,1)S(1)}, bf16[64,4096]{1,0:T(8,128)(2,1)}, u32[]{:S(2)}) copy-start(bf16[64,4096]{1,0:T(8,128)(2,1)} %all-reduce.2.cloned.1.call-done) | copy-start | bytes 1572868
  166.4 8.7 %copy-start.15 = (bf16[1,64,4096]{2,1,0:T(8,128)(2,1)S(1)}, bf16[1,64,4096]{2,1,0:T(8,128)(2,1)}, u32[]{:S(2)}) copy-start(bf16[1,64,4096]{2,1,0:T(8,128)(2,1)} %get-tuple-element.114) | copy-start | bytes 1572868 | tf_op jit(solution)/shard_map/while
  179.0 8.7 %copy-start.15 = (bf16[1,64,4096]{2,1,0:T(8,128)(2,1)S(1)}, bf16[1,64,4096]{2,1,0:T(8,128)(2,1)}, u32[]{:S(2)}) copy-start(bf16[1,64,4096]{2,1,0:T(8,128)(2,1)} %get-tuple-element.114) | copy-start | bytes 1572868 | tf_op jit(solution)/shard_map/while
  191.5 8.7 %copy-start.15 = (bf16[1,64,4096]{2,1,0:T(8,128)(2,1)S(1)}, bf16[1,64,4096]{2,1,0:T(8,128)(2,1)}, u32[]{:S(2)}) copy-start(bf16[1,64,4096]{2,1,0:T(8,128)(2,1)} %get-tuple-element.114) | copy-start | bytes 1572868 | tf_op jit(solution)/shard_map/while
  204.0 8.7 %copy-start.15 = (bf16[1,64,4096]{2,1,0:T(8,128)(2,1)S(1)}, bf16[1,64,4096]{2,1,0:T(8,128)(2,1)}, u32[]{:S(2)}) copy-start(bf16[1,64,4096]{2,1,0:T(8,128)(2,1)} %get-tuple-element.114) | copy-start | bytes 1572868 | tf_op jit(solution)/shard_map/while
  216.5 8.7 %copy-start.15 = (bf16[1,64,4096]{2,1,0:T(8,128)(2,1)S(1)}, bf16[1,64,4096]{2,1,0:T(8,128)(2,1)}, u32[]{:S(2)}) copy-start(bf16[1,64,4096]{2,1,0:T(8,128)(2,1)} %get-tuple-element.114) | copy-start | bytes 1572868 | tf_op jit(solution)/shard_map/while
  229.0 8.7 %copy-start.15 = (bf16[1,64,4096]{2,1,0:T(8,128)(2,1)S(1)}, bf16[1,64,4096]{2,1,0:T(8,128)(2,1)}, u32[]{:S(2)}) copy-start(bf16[1,64,4096]{2,1,0:T(8,128)(2,1)} %get-tuple-element.114) | copy-start | bytes 1572868 | tf_op jit(solution)/shard_map/while
  241.5 8.7 %copy-start.15 = (bf16[1,64,4096]{2,1,0:T(8,128)(2,1)S(1)}, bf16[1,64,4096]{2,1,0:T(8,128)(2,1)}, u32[]{:S(2)}) copy-start(bf16[1,64,4096]{2,1,0:T(8,128)(2,1)} %get-tuple-element.114) | copy-start | bytes 1572868 | tf_op jit(solution)/shard_map/while
  254.0 8.7 %copy-start.15 = (bf16[1,64,4096]{2,1,0:T(8,128)(2,1)S(1)}, bf16[1,64,4096]{2,1,0:T(8,128)(2,1)}, u32[]{:S(2)}) copy-start(bf16[1,64,4096]{2,1,0:T(8,128)(2,1)} %get-tuple-element.114) | copy-start | bytes 1572868 | tf_op jit(solution)/shard_map/while
  288.5 5.3 %copy-start.8 = (bf16[2,2048]{1,0:T(2,128)(2,1)S(1)}, bf16[2,2048]{1,0:T(2,128)(2,1)}, u32[]{:S(2)}) copy-start(bf16[2,2048]{1,0:T(2,128)(2,1)} %param.17) | copy-start | bytes 24580
  288.5 5.3 %copy-start.9 = (f32[3,64]{1,0:T(4,128)S(1)}, f32[3,64]{1,0:T(4,128)}, u32[]{:S(2)}) copy-start(f32[3,64]{1,0:T(4,128)} %param.24) | copy-start | bytes 2308
  288.5 5.3 %copy-start.11 = (bf16[3,64,2]{1,2,0:T(2,128)(2,1)S(1)}, bf16[3,64,2]{1,2,0:T(2,128)(2,1)}, u32[]{:S(2)}) copy-start(bf16[3,64,2]{1,2,0:T(2,128)(2,1)} %param.23) | copy-start | bytes 2308
  288.5 98.7 %all-to-all-start = ((bf16[8,4,64,2048]{3,2,1,0:T(8,128)(2,1)}), bf16[8,4,64,2048]{3,2,1,0:T(8,128)(2,1)}, u32[]{:S(2)}, u32[]{:S(2)}) async-start(bf16[8,4,64,2048]{3,2,1,0:T(8,128)(2,1)} %stack.8), calls=%async_computation | async-start | bytes 16777216 | tf_op jit(solution)/shard_map/all_to_all | solution.py:112
  387.2 8.4 %copy-start.13 = (bf16[3,64,4,512]{3,2,1,0:T(4,128)(2,1)S(1)}, bf16[3,64,4,512]{3,2,1,0:T(4,128)(2,1)}, u32[]{:S(2)}) copy-start(bf16[3,64,4,512]{3,2,1,0:T(4,128)(2,1)} %param.22) | copy-start | bytes 2359300
  395.5 5.3 %copy-start.2 = (f32[3,64,2048]{2,1,0:T(8,128)S(1)}, f32[3,64,2048]{2,1,0:T(8,128)}, u32[]{:S(2)}) copy-start(f32[3,64,2048]{2,1,0:T(8,128)} %convolution_add_fusion) | copy-start | bytes 4718596
Sparse Core Ops, SparseCore 0:
  19.6 143.1 all-reduce.1
